TPU v7x, 512 devices: a whole 4x4x16 slice. The times are simulated.
512 devices in a mesh: row: 32 (over z, core), col: 16 (over x, y).
Axes of the slice: x: 4, y: 4, z: 16, core: 2. Of those that a mesh axis runs over, the one named last changes fastest.
Arguments:
- trailing: float32 [16384, 16384], P('row', 'col'), may hold values from -6 to 6
- panel: float32 [16384, 512], P(('row', 'col')), may hold values from -0.25 to 0.25
- inv_factor: float32 [512, 512], P(None, 'col'), as said below
- later_series: float32 [16384, 1024], P('row', 'col'), may hold values from -6 to 6
- fold_series: float32 [512, 1024], P('row', 'col'), may hold values from -6 to 6
- fold_len: int32 [1024], P('col'), may hold values from 1 to 32, as said below
Outputs:
- new_trailing: float32 [16384, 16384], P('row', 'col')
- new_series: float32 [16384, 1024], P('row', 'col')
Inputs may be any that keep to these rules, and one draw needn't show every extreme that they name: inv_factor is lower triangular with a diagonal between 1 and 2. `fold_len`: some series reach all 32 blocks and some only one.
All inputs are finite; a program needn't handle non-finite values.
Results may differ from a plain program's by a relative error of at most 0.0003.
Values sent between devices are 32-bit elements; how exact they have to be, the bound alone decides.
No kernel may reach another device: no remote copies, remote signals or barrier semaphores. Data moves between devices by JAX's collectives and lax.ppermute only.
A program may use at most 64 MiB of HBM per device.

v0:
```python
import jax
import jax.numpy as jnp
from jax import lax
from jax.sharding import PartitionSpec as P


def spread(array, axis, root):
    mine = lax.axis_index(axis) == root
    return lax.psum(jnp.where(mine, array, jnp.zeros_like(array)), axis)


def on_device(trailing, panel, inv_factor, later_series, fold_series, fold_len):
    highest = lax.Precision.HIGHEST
    contract = (((1,), (1,)), ((), ()))
    inverse = lax.all_gather(inv_factor, "col", axis=1, tiled=True)
    solved_mine = lax.dot_general(
        panel, inverse, contract, precision=highest, preferred_element_type=jnp.float32
    )
    row_block = lax.all_gather(solved_mine, "col", axis=0, tiled=True)
    rows_here = trailing.shape[0]
    cols_here = trailing.shape[1]
    tiles_across = cols_here // rows_here
    row_pos = lax.axis_index("row")
    col_pos = lax.axis_index("col")
    pieces = []
    for offset in range(tiles_across):
        source = col_pos * tiles_across + offset
        pieces.append(spread(row_block, "row", source))
    col_panel = jnp.concatenate(pieces, 0)
    update = lax.dot_general(
        row_block, col_panel, contract, precision=highest, preferred_element_type=jnp.float32
    )
    col_tile = (col_pos * cols_here + jnp.arange(cols_here, dtype=jnp.int32)) // rows_here
    lower = col_tile <= row_pos
    new_trailing = jnp.where(lower[None, :], trailing - update, trailing)
    fold_all = lax.all_gather(fold_series, "row", axis=0, tiled=True)
    innovations = jnp.dot(inverse, fold_all, precision=highest, preferred_element_type=jnp.float32)
    correction = jnp.dot(
        row_block, innovations, precision=highest, preferred_element_type=jnp.float32
    )
    active = row_pos < fold_len
    new_series = jnp.where(active[None, :], later_series - correction, later_series)
    return (new_trailing, new_series)


def solution(mesh):
    in_specs = (
        P("row", "col"),
        P(("row", "col"), None),
        P(None, "col"),
        P("row", "col"),
        P("row", "col"),
        P("col"),
    )
    out_specs = (P("row", "col"), P("row", "col"))
    return jax.shard_map(
        on_device, mesh=mesh, in_specs=in_specs, out_specs=out_specs, check_vma=False
    )
```

profile of v0, /device:TPU:1, one launch (start us, length us, event | category | flops | bytes accessed | tf_op | source)
XLA Modules:
  0.0 367.0 jit_solution(11055402713785752273)
XLA Ops:
  7.2 0.0 copy-start
  7.2 0.0 all-gather.3.cloned.1.call-start
  7.2 0.7 all-gather.3.cloned.1.call-update
  7.9 0.0 all-gather.5.cloned.1.call-start
  8.0 64.4 %all-gather.3.cloned.1.call-done = f32[512,512]{0,1:T(8,128)} async-done(((f32[512,32]{0,1:T(8,128)}), f32[512,512]{0,1:T(8,128)}) %all-gather.3.cloned.1.call-update) | async-done | bytes 1048592 | tf_op jit(solution)/shard_map/all_gather | solution.py:15
  72.3 0.0 copy-done
  72.3 2.6 fusion.12
  74.9 0.0 all-gather.5.cloned.1.call-update
  74.9 0.0 all-reduce.3.cloned.1.call-start
  75.0 0.0 copy-start.4
  75.0 0.0 copy-start.5
  75.0 0.0 copy-start.2
  75.0 58.2 %all-gather.5.cloned.1.call-done = f32[512,512]{1,0:T(8,128)} async-done(((f32[32,512]{1,0:T(8,128)}), f32[512,512]{1,0:T(8,128)}) %all-gather.5.cloned.1.call-update) | async-done | bytes 1048592 | tf_op jit(solution)/shard_map/all_gather | solution.py:19
  133.2 2.8 broadcast_select_fusion.1
  136.0 0.0 all-reduce.3.cloned.1.call-update
  136.1 0.0 copy-done.4
  136.1 34.2 %all_gather.11 = f32[512,64]{1,0:T(8,128)S(1)} all-gather(f32[16,64]{1,0:T(8,128)S(1)} %copy-done.4), channel_id=1, replica_groups=mesh['row'=32,'col'=16] {'row'}, dimensions={0}, use_global_device_ids=true | all-gather | bytes 135168 | tf_op jit(solution)/shard_map/all_gather | solution.py:36
  170.3 0.0 copy-done.5
  170.3 0.0 copy-done.2
  170.3 1.8 fusion.13
  172.1 0.0 copy-done.1
  172.1 1.8 fusion.6
  174.0 179.8 %all-reduce.3.cloned.1.call-done = (f32[512,512]{1,0:T(8,128)}, f32[512,512]{1,0:T(8,128)}) async-done(((f32[512,512]{1,0:T(8,128)}, f32[512,512]{1,0:T(8,128)}), (f32[512,512]{1,0:T(8,128)}, f32[512,512]{1,0:T(8,128)})) %all-reduce.3.cloned.1.call-update) | async-done | bytes 2097168 | tf_op jit(solution)/shard_map/psum | solution.py:9
  353.7 6.7 %subtract_select_fusion = f32[512,1024]{1,0:T(8,128)} fusion(f32[512,1024]{1,0:T(8,128)} %param.6, f32[512,512]{1,0:T(8,128)S(1)} %copy-done.1, f32[512,512]{1,0:T(8,128)} %get-tuple-element.2, f32[512,512]{1,0:T(8,128)} %get-tuple-element.3, pred[1024]{0:T(1024)(128)(4,1)S(1)} %fusion.8), kind=kOutput, calls=%fused_computation | convolution fusion | flops 3222798336 | bytes 7341056 | tf_op jit(solution)/shard_map/dot_general | solution.py:30
  (5 shorter events, 0.0 us)
Async XLA Ops:
  7.2 65.2 %copy-start = (f32[32,512]{1,0:T(8,128)S(1)}, f32[32,512]{1,0:T(8,128)}, u32[]{:S(2)}) copy-start(f32[32,512]{1,0:T(8,128)} %param.7) | copy-start | bytes 196612
  7.2 65.1 %all-gather.3.cloned.1.call-start = ((), (), s32[]{:S(2)}) async-start(), calls=%async_computation | async-start | bytes 1114112 | tf_op jit(solution)/shard_map/all_gather | solution.py:15
  7.9 125.3 %all-gather.5.cloned.1.call-start = ((), (), s32[]{:S(2)}) async-start(), calls=%async_computation.1 | async-start | bytes 1114112 | tf_op jit(solution)/shard_map/all_gather | solution.py:19
  74.9 278.8 %all-reduce.3.cloned.1.call-start = ((), (), s32[]{:S(2)}) async-start(), calls=%async_computation.2 | async-start | bytes 4194304 | tf_op jit(solution)/shard_map/psum | solution.py:9
  75.0 61.1 %copy-start.4 = (f32[16,64]{1,0:T(8,128)S(1)}, f32[16,64]{1,0:T(8,128)}, u32[]{:S(2)}) copy-start(f32[16,64]{1,0:T(8,128)} %param.10) | copy-start | bytes 12292
  75.0 95.3 %copy-start.5 = (s32[64]{0:T(128)S(1)}, s32[64]{0:T(128)}, u32[]{:S(2)}) copy-start(s32[64]{0:T(128)} %param.11) | copy-start | bytes 772
  75.0 95.3 %copy-start.2 = (f32[512,512]{0,1:T(8,128)S(1)}, f32[512,512]{0,1:T(8,128)}, u32[]{:S(2)}) copy-start(f32[512,512]{0,1:T(8,128)} %all-gather.3.cloned.1.call-done) | copy-start | bytes 3145732
  136.0 36.1 %copy-start.1 = (f32[512,512]{1,0:T(8,128)S(1)}, f32[512,512]{1,0:T(8,128)}, u32[]{:S(2)}) copy-start(f32[512,512]{1,0:T(8,128)} %all-gather.5.cloned.1.call-done) | copy-start | bytes 3145732
  136.0 36.1 %copy-start.3 = (f32[512,64]{0,1:T(8,128)S(1)}, f32[512,64]{0,1:T(8,128)}, u32[]{:S(2)}) copy-start(f32[512,64]{0,1:T(8,128)} %param.9) | copy-start | bytes 393220
Sparse Core Ops, SparseCore 0:
  11.0 61.2 all-gather.2
  75.9 57.2 all-gather.4
  136.2 217.5 all-reduce.2
where the time goes:
time: 367 us
  waiting for transfers between devices  303 us (83%)
  blocking collectives  34.2 us (9%)
  between operations  13.8 us (4%)
  matrix products  12.9 us (4%)
    psum x1, waiting for transfers between devices, spread(): return lax.psum(jnp.where(mine, array, jnp.zeros_like(array)), axis)  180 us
    all_gather x1, waiting for transfers between devices, on_device(): inverse = lax.all_gather(inv_factor, 'col', axis=1, tiled=True)  64.4 us
    all_gather x1, waiting for transfers between devices, on_device(): row_block = lax.all_gather(solved_mine, 'col', axis=0, tiled=True)  58.2 us
    all_gather x1, blocking collectives, on_device(): fold_all = lax.all_gather(fold_series, 'row', axis=0, tiled=True)  34.2 us
  transfers between devices with their start and end apart: 3, of which 3 were waited for; matrix products, arithmetic and copies ran while one was open for 1% of the time, Pallas kernels for 0%

commit v1 on v0

--- a/solution.py
+++ b/solution.py
@@ -2,6 +2,18 @@
 import jax.numpy as jnp
 from jax import lax
 from jax.sharding import PartitionSpec as P
+
+
+def review_space_in(u, chip_axis):
+    return jnp.concatenate(
+        jax.lax.all_to_all(
+            jnp.stack(jax.lax.axis_size(chip_axis) * [u]),
+            split_axis=0,
+            concat_axis=0,
+            axis_name=chip_axis,
+        ),
+        0,
+    )
 
 
 def spread(array, axis, root):
@@ -16,7 +28,7 @@
     solved_mine = lax.dot_general(
         panel, inverse, contract, precision=highest, preferred_element_type=jnp.float32
     )
-    row_block = lax.all_gather(solved_mine, "col", axis=0, tiled=True)
+    row_block = review_space_in(solved_mine, "col")
     rows_here = trailing.shape[0]
     cols_here = trailing.shape[1]
     tiles_across = cols_here // rows_here

time: 367 us -> 327 us (0.89)
  waiting for transfers between devices: 303 us -> 258 us
  starting transfers between devices: 0.12 us -> 4.45 us
    all_gather x1 -> x0, waiting for transfers between devices: 58.2 us -> none  [on_device(): row_block = lax.all_gather(solved_mine, 'col', axis=0, tiled=True)]
    all_to_all x0 -> x1, waiting for transfers between devices: none -> 14.2 us  [review_space_in(): jax.lax.all_to_all(jnp.stack(jax.lax.axis_size(chip_axis) * [u]), split_a...]
    all_to_all x0 -> x1, starting transfers between devices: none -> 4.37 us  [review_space_in(): jax.lax.all_to_all(jnp.stack(jax.lax.axis_size(chip_axis) * [u]), split_a...]
where the time goes in v1:
time: 327 us
  waiting for transfers between devices  258 us (79%)
  blocking collectives  35.5 us (11%)
  between operations  14.1 us (4%)
  matrix products  12.2 us (4%)
  starting transfers between devices  4.45 us (1%)
    psum x1, waiting for transfers between devices, spread(): return lax.psum(jnp.where(mine, array, jnp.zeros_like(array)), axis)  179 us
    all_gather x1, waiting for transfers between devices, on_device(): inverse = lax.all_gather(inv_factor, 'col', axis=1, tiled=True)  64.4 us
    all_gather x1, blocking collectives, on_device(): fold_all = lax.all_gather(fold_series, 'row', axis=0, tiled=True)  35.5 us
    all_to_all x1, waiting for transfers between devices, review_space_in(): jax.lax.all_to_all(jnp.stack(jax.lax.axis_size(chip_axis) * [u]), split_a...  14.2 us
    dot_general x1, matrix products, on_device(): lax.dot_general(row_block, col_panel, contract, precision=highest, prefer...  6.69 us
  transfers between devices with their start and end apart: 3, of which 3 were waited for; matrix products, arithmetic and copies ran while one was open for 1% of the time, Pallas kernels for 0%

profile of v1, /device:TPU:1, one launch (start us, length us, event | category | flops | bytes accessed | tf_op | source)
XLA Modules:
  0.0 327.0 jit_solution(6694178178313173914)
XLA Ops:
  7.2 0.0 copy-start
  7.2 0.0 all-gather.2.cloned.1.call-start
  7.2 0.7 all-gather.2.cloned.1.call-update
  7.9 64.4 %all-gather.2.cloned.1.call-done = f32[512,512]{0,1:T(8,128)} async-done(((f32[512,32]{0,1:T(8,128)}), f32[512,512]{0,1:T(8,128)}) %all-gather.2.cloned.1.call-update) | async-done | bytes 1048592 | tf_op jit(solution)/shard_map/all_gather | solution.py:27
  72.3 0.0 copy-done
  72.3 1.9 fusion.12
  74.3 1.1 stack.2
  75.4 4.4 %all-to-all-start = ((f32[16,32,512]{2,1,0:T(8,128)}), f32[16,32,512]{2,1,0:T(8,128)S(1)}, u32[]{:S(2)}, u32[]{:S(2)}) async-start(f32[16,32,512]{2,1,0:T(8,128)} %stack.2), calls=%async_computation | async-start | bytes 2097152 | tf_op jit(solution)/shard_map/all_to_all | solution.py:9
  79.7 0.0 all-reduce.3.cloned.1.call-start
  79.8 0.0 copy-start.3
  79.8 0.0 copy-start.4
  79.8 0.0 copy-start.1
  79.8 14.2 %all-to-all-done = f32[16,32,512]{2,1,0:T(8,128)S(1)} async-done(((f32[16,32,512]{2,1,0:T(8,128)}), f32[16,32,512]{2,1,0:T(8,128)S(1)}, u32[]{:S(2)}, u32[]{:S(2)}) %all-to-all-start) | async-done | bytes 1048608 | tf_op jit(solution)/shard_map/all_to_all | solution.py:9
  94.0 1.6 broadcast_select_fusion.1
  95.6 0.0 all-reduce.3.cloned.1.call-update
  95.6 0.0 copy-done.3
  95.6 35.5 %all_gather.7 = f32[512,64]{1,0:T(8,128)S(1)} all-gather(f32[16,64]{1,0:T(8,128)S(1)} %copy-done.3), channel_id=1, replica_groups=mesh['row'=32,'col'=16] {'row'}, dimensions={0}, use_global_device_ids=true | all-gather | bytes 135168 | tf_op jit(solution)/shard_map/all_gather | solution.py:48
  131.2 0.0 copy-done.4
  131.2 0.0 copy-done.1
  131.2 1.8 fusion.13
  133.0 0.0 copy-done.2
  133.0 1.8 fusion.6
  134.8 178.6 %all-reduce.3.cloned.1.call-done = (f32[512,512]{1,0:T(8,128)}, f32[512,512]{1,0:T(8,128)}) async-done(((f32[512,512]{1,0:T(8,128)}, f32[512,512]{1,0:T(8,128)}), (f32[512,512]{1,0:T(8,128)}, f32[512,512]{1,0:T(8,128)})) %all-reduce.3.cloned.1.call-update) | async-done | bytes 2097168 | tf_op jit(solution)/shard_map/psum | solution.py:21
  313.4 6.7 %subtract_select_fusion = f32[512,1024]{1,0:T(8,128)} fusion(f32[512,1024]{1,0:T(8,128)} %param.6, f32[512,512]{1,0:T(8,128)S(1)} %bitcast.11, f32[512,512]{1,0:T(8,128)} %get-tuple-element.2, f32[512,512]{1,0:T(8,128)} %get-tuple-element.3, pred[1024]{0:T(1024)(128)(4,1)S(1)} %fusion.8), kind=kOutput, calls=%fused_computation | convolution fusion | flops 3222798336 | bytes 7341056 | tf_op jit(solution)/shard_map/dot_general | solution.py:42
  (3 shorter events, 0.0 us)
Async XLA Ops:
  7.2 65.2 %copy-start = (f32[32,512]{1,0:T(8,128)S(1)}, f32[32,512]{1,0:T(8,128)}, u32[]{:S(2)}) copy-start(f32[32,512]{1,0:T(8,128)} %param.7) | copy-start | bytes 196612
  7.2 65.1 %all-gather.2.cloned.1.call-start = ((), (), s32[]{:S(2)}) async-start(), calls=%async_computation.1 | async-start | bytes 1114112 | tf_op jit(solution)/shard_map/all_gather | solution.py:27
  75.4 18.7 %all-to-all-start = ((f32[16,32,512]{2,1,0:T(8,128)}), f32[16,32,512]{2,1,0:T(8,128)S(1)}, u32[]{:S(2)}, u32[]{:S(2)}) async-start(f32[16,32,512]{2,1,0:T(8,128)} %stack.2), calls=%async_computation | async-start | bytes 2097152 | tf_op jit(solution)/shard_map/all_to_all | solution.py:9
  79.7 233.7 %all-reduce.3.cloned.1.call-start = ((), (), s32[]{:S(2)}) async-start(), calls=%async_computation.2 | async-start | bytes 4194304 | tf_op jit(solution)/shard_map/psum | solution.py:21
  79.8 15.8 %copy-start.3 = (f32[16,64]{1,0:T(8,128)S(1)}, f32[16,64]{1,0:T(8,128)}, u32[]{:S(2)}) copy-start(f32[16,64]{1,0:T(8,128)} %param.10) | copy-start | bytes 12292
  79.8 51.3 %copy-start.4 = (s32[64]{0:T(128)S(1)}, s32[64]{0:T(128)}, u32[]{:S(2)}) copy-start(s32[64]{0:T(128)} %param.11) | copy-start | bytes 772
  79.8 51.4 %copy-start.1 = (f32[512,512]{0,1:T(8,128)S(1)}, f32[512,512]{0,1:T(8,128)}, u32[]{:S(2)}) copy-start(f32[512,512]{0,1:T(8,128)} %all-gather.2.cloned.1.call-done) | copy-start | bytes 3145732
  95.6 37.4 %copy-start.2 = (f32[512,64]{0,1:T(8,128)S(1)}, f32[512,64]{0,1:T(8,128)}, u32[]{:S(2)}) copy-start(f32[512,64]{0,1:T(8,128)} %param.9) | copy-start | bytes 393220
Sparse Core Ops, SparseCore 0:
  11.0 61.2 all-gather.1
  95.7 217.6 all-reduce.2
